TPU v7x, 128 devices: a whole 4x4x4 slice. The times are simulated.
128 devices in a mesh: tm: 16 (over x, z_hi, core), freq: 8 (over y, z_lo).
Axes of the slice: x: 4, y: 4, z: 4 (z_hi: 2, z_lo: 2; z = z_hi * 2 + z_lo), core: 2. Of those that a mesh axis runs over, the one named last changes fastest.
Arguments:
- visibility: bfloat16 [2, 32, 1024, 4096], P(None, None, 'freq', 'tm'), may hold values from -6 to 6
- spectrum_power_sum: float32 [1024, 4096], P('freq', 'tm'), may hold values from 50 to 500, as said below
- square_sum: float32 [1024, 4096], P('freq', 'tm'), as said below
- accum_count: int32 [1024, 4096], P('freq', 'tm'), may hold values from 64 to 256
- rfi_mask: int32 [1024, 4096], P('freq', 'tm'), may hold values 0 or 1
- baseline_delay_class: int32 [32, 1], P('freq'), may hold values from 0 to 3
- filter_bank: bfloat16 [4, 1024, 1024], replicated, may hold values from -0.1875 to 0.1875
Outputs:
- filtered: bfloat16 [2, 32, 1024, 4096], P(None, 'freq', None, 'tm')
Inputs may be any that keep to these rules, and one draw needn't show every extreme that they name: `spectrum_power_sum`: positive in every sample. `square_sum`: positive in every sample.
All inputs are finite; a program needn't handle non-finite values. No bound on the sum of `rfi_mask` on one device may be relied on, other than what follows from the above.
Results may differ from a plain program's by a relative error of at most 0.0043.
The roundings to bfloat16 on the way count: a program that leaves them out, or rounds other values in their place, can miss the bound.
Values may be sent and summed in bfloat16 or wider, within the bound.
A program may use at most 128 MiB of HBM per device.

v0:
```python
import math

import jax
import jax.numpy as jnp
from jax import lax
from jax.sharding import PartitionSpec as P

RIM = 16


def padded_2(value, sides, width):
    for axis, dim in sides:
        devices, length = (lax.axis_size(axis), value.shape[dim])
        up = [(i, (i + 1) % devices) for i in range(devices)]
        down = [(j, i) for i, j in up]
        last = lax.slice_in_dim(value, length - width, length, axis=dim)
        leading = lax.slice_in_dim(value, 0, width, axis=dim)
        before = lax.ppermute(last, axis, up)
        after = lax.ppermute(leading, axis, down)
        value = jnp.concatenate([before, value, after], axis=dim)
    return value


def rotation_table(rows_n, cols_n, period):
    row_index = jnp.arange(rows_n, dtype=jnp.int32)
    col_index = jnp.arange(cols_n, dtype=jnp.int32)
    phase = row_index[:, None] * col_index[None, :] % period
    angles = 2.0 * math.pi / period * phase.astype(jnp.float32)
    cosine = jnp.cos(angles)
    sine = jnp.sin(angles)
    real_row = jnp.stack([cosine, sine])
    imag_row = jnp.stack([-sine, cosine])
    return jnp.stack([real_row, imag_row])


def twist_table(rows_n, cols_n, period):
    row_index = jnp.arange(rows_n, dtype=jnp.int32)
    col_index = jnp.arange(cols_n, dtype=jnp.int32)
    phase = row_index[:, None] * col_index[None, :] % period
    angles = 2.0 * math.pi / period * phase.astype(jnp.float32)
    return (jnp.cos(angles), jnp.sin(angles))


def sidereal_transform(received):
    periods = lax.axis_size("tm")
    samples = received.shape[3]
    inner_len = samples // periods
    base_n = received.shape[1]
    chan_n = received.shape[2]
    widened = received.astype(jnp.float32).reshape(2, base_n, chan_n, periods, inner_len)
    better = lax.Precision.HIGH
    first_table = rotation_table(periods, periods, periods)
    stepped = jnp.einsum("cbfps,dcjp->dbfjs", widened, first_table, precision=better)
    cos_two, sin_two = twist_table(periods, inner_len, samples)
    twist_real = stepped[0] * cos_two + stepped[1] * sin_two
    twist_imag = stepped[1] * cos_two - stepped[0] * sin_two
    twisted = jnp.stack([twist_real, twist_imag])
    tertiary_lookup = rotation_table(inner_len, inner_len, inner_len)
    finished = jnp.einsum("cbfjs,dcks->dbfkj", twisted, tertiary_lookup, precision=better)
    norm_scale = 1.0 / math.sqrt(samples)
    finished = finished.reshape(2, base_n, chan_n, samples) * norm_scale
    return finished.astype(jnp.bfloat16)


def shards(
    visibility,
    spectrum_power_sum,
    square_sum,
    accum_count,
    rfi_mask,
    baseline_delay_class,
    filter_bank,
):
    counts = accum_count.astype(jnp.float32)
    kurtosis = (
        (counts + 1.0)
        / (counts - 1.0)
        * (counts * square_sum / (spectrum_power_sum * spectrum_power_sum) - 1.0)
    )
    flag_weight = rfi_mask.astype(jnp.float32) * jnp.exp(-2.0 * (kurtosis - 1.0) ** 2)
    local_len = flag_weight.shape[1]
    padded = padded_2(flag_weight, (("tm", 1),), RIM)
    smooth_weight = jnp.zeros(flag_weight.shape, jnp.float32)
    for offset in range(2 * RIM + 1):
        factor = (RIM + 1 - abs(offset - RIM)) / float((RIM + 1) ** 2)
        smooth_weight = smooth_weight + factor * padded[:, offset : offset + local_len]
    weighted = (visibility.astype(jnp.float32) * smooth_weight[None, None]).astype(jnp.bfloat16)
    spectrum = sidereal_transform(
        lax.all_to_all(weighted, "tm", split_axis=2, concat_axis=3, tiled=True)
    )
    chosen = jnp.take(filter_bank, baseline_delay_class[:, 0], axis=0)
    moved = lax.all_to_all(spectrum, "tm", split_axis=3, concat_axis=2, tiled=True)
    return jnp.einsum(
        "bgf,cbfm->cbgm",
        chosen,
        lax.all_to_all(moved, "freq", split_axis=1, concat_axis=2, tiled=True),
        preferred_element_type=jnp.float32,
    ).astype(jnp.bfloat16)


def solution(mesh):
    in_specs = (
        P(None, None, "freq", "tm"),
        P("freq", "tm"),
        P("freq", "tm"),
        P("freq", "tm"),
        P("freq", "tm"),
        P("freq", None),
        P(),
    )
    out_specs = P(None, "freq", None, "tm")
    return jax.shard_map(shards, mesh=mesh, in_specs=in_specs, out_specs=out_specs, check_vma=False)
```

profile of v0, /device:TPU:1, one launch (start us, length us, event | category | flops | bytes accessed | tf_op | source)
XLA Modules:
  0.0 342.4 jit_solution(15936010906509529654)
XLA Ops:
  1.3 5.0 %collective-permute-start = (f32[128,16]{1,0:T(8,128)S(1)}, f32[128,16]{1,0:T(8,128)S(1)}, u32[]{:S(2)}, u32[]{:S(2)}) collective-permute-start(f32[128,16]{1,0:T(8,128)S(1)} %get-tuple-element.11), channel_id=1, source_target_pairs={{0,8},{8,16},{16,24},{24,32},{32,40},{40,48},{48,56},{56,64},{64,7... | collective-permute-start | bytes 24584 | tf_op jit(solution)/shard_map/ppermute | solution.py:18
  7.6 3.9 %collective-permute-done.1 = f32[128,16]{1,0:T(8,128)S(1)} collective-permute-done((f32[128,16]{1,0:T(8,128)S(1)}, f32[128,16]{1,0:T(8,128)S(1)}, u32[]{:S(2)}, u32[]{:S(2)}) %collective-permute-start.1) | collective-permute-done | bytes 8224 | tf_op jit(solution)/shard_map/ppermute | solution.py:19
  11.5 1.7 fusion.33
  13.2 7.2 %multiply_convert_fusion = bf16[2,32,128,256]{3,1,0,2:T(8,128)(2,1)} fusion(bf16[2,32,128,256]{3,2,1,0:T(8,128)(2,1)} %param.7, f32[128,256]{1,0:T(8,128)S(1)} %fusion.33), kind=kLoop, calls=%fused_computation.13 | loop fusion | flops 6291456 | bytes 8519680 | tf_op jit(solution)/shard_map/convert_element_type | solution.py:87
  20.3 5.5 %all-to-all-start = ((bf16[2,32,128,256]{3,1,0,2:T(8,128)(2,1)}), bf16[2,32,128,256]{3,1,0,2:T(8,128)(2,1)}, u32[]{:S(2)}, u32[]{:S(2)}) async-start(bf16[2,32,128,256]{3,1,0,2:T(8,128)(2,1)} %multiply_convert_fusion), calls=%async_computation | async-start | bytes 8388608 | tf_op jit(solution)/shard_map/all_to_all | solution.py:89
  28.2 50.4 %all-to-all-done = bf16[2,32,128,256]{3,1,0,2:T(8,128)(2,1)} async-done(((bf16[2,32,128,256]{3,1,0,2:T(8,128)(2,1)}), bf16[2,32,128,256]{3,1,0,2:T(8,128)(2,1)}, u32[]{:S(2)}, u32[]{:S(2)}) %all-to-all-start) | async-done | bytes 4194336 | tf_op jit(solution)/shard_map/all_to_all | solution.py:89
  78.5 9.8 %fusion.15 = f32[2,32,8,16,256]{4,3,2,1,0:T(8,128)S(1)} fusion(bf16[2,32,16,8,256]{4,1,0,3,2:T(8,128)(2,1)} %bitcast.8, f32[1,2,16,16]{3,2,1,0:T(8,128)S(1)} %get-tuple-element.14, f32[1,2,16,16]{3,2,1,0:T(8,128)S(1)} %get-tuple-element.13), kind=kOutput, calls=%fused_computation.23 | convolution fusion | flops 402654208 | bytes 12587008 | tf_op jit(solution)/shard_map/cbfps,dcjp->dbfjs/dot_general | solution.py:53
  88.3 1.9 multiply_add_fusion
  90.3 1.8 pad_maximum_fusion
  92.1 11.1 %fusion.10 = bf16[2,32,8,256,16]{3,1,4,2,0:T(8,128)(2,1)} fusion(f32[2,32,8,16,256]{4,3,2,1,0:T(8,128)S(1)} %pad_maximum_fusion, f32[1,2,256,256]{3,2,1,0:T(8,128)S(1)} %get-tuple-element.10, f32[1,2,256,256]{3,2,1,0:T(8,128)S(1)} %get-tuple-element.9), kind=kOutput, calls=%fused_computation.15 | convolution fusion | flops 6446907392 | bytes 13631488 | tf_op jit(solution)/shard_map/cbfjs,dcks->dbfkj/dot_general | solution.py:59
  103.1 23.2 %copy.33 = bf16[2,32,8,256,16]{1,2,0,4,3:T(8,128)(2,1)} copy(bf16[2,32,8,256,16]{3,1,4,2,0:T(8,128)(2,1)} %fusion.10) | data formatting | bytes 8388608 | tf_op jit(solution)/shard_map/convert_element_type | solution.py:62
  126.3 20.7 %reshape.226 = bf16[16,2,65536]{2,1,0:T(2,128)(2,1)} reshape(bf16[4096,2,8,32]{3,2,1,0:T(8,128)(2,1)} %bitcast.74) | data formatting | bytes 8388608
  147.1 63.5 %all_to_all.51 = bf16[16,2,65536]{2,1,0:T(2,128)(2,1)} all-to-all(bf16[16,2,65536]{2,1,0:T(2,128)(2,1)} %reshape.226), channel_id=1, replica_groups=mesh['tm'=16,'freq'=8] {'tm'}, dimensions={0} | all-to-all | bytes 8388608 | tf_op jit(solution)/shard_map/all_to_all | solution.py:92
  210.6 16.0 %reshape.227 = bf16[4096,2,8,32]{3,2,1,0:T(8,128)(2,1)} reshape(bf16[16,2,65536]{2,1,0:T(2,128)(2,1)} %all_to_all.51) | data formatting | bytes 8388608
  226.6 19.5 %copy.22 = bf16[2,32,16,8,256]{4,3,2,0,1:T(8,128)(2,1)} copy(bf16[2,32,16,8,256]{1,3,0,4,2:T(8,128)(2,1)} %bitcast.75) | data formatting | bytes 8388608 | tf_op jit(solution)/shard_map/all_to_all | solution.py:92
  246.1 5.4 %all-to-all-start.2 = ((bf16[2,32,128,256]{3,2,0,1:T(8,128)(2,1)}), bf16[2,32,128,256]{3,2,0,1:T(8,128)(2,1)}, u32[]{:S(2)}, u32[]{:S(2)}) async-start(bf16[2,32,128,256]{3,2,0,1:T(8,128)(2,1)} %bitcast.76), calls=%async_computation.2 | async-start | bytes 8388608 | tf_op jit(solution)/shard_map/all_to_all | solution.py:96
  251.6 5.9 %fusion.151 = (bf16[4,512,1024]{2,1,0:T(8,128)(2,1)}, bf16[4,512,1024]{2,1,0:T(8,128)(2,1)}) fusion(bf16[4,1024,1024]{2,1,0:T(8,128)(2,1)} %param.13), kind=kLoop, calls=%fused_computation.234 | loop fusion | bytes 16777216 | tf_op jit(solution)/shard_map/jit(_take)/gather | solution.py:91
  257.5 5.0 %gather_fusion = bf16[4,512,1024]{2,1,0:T(8,128)(2,1)} fusion(bf16[4,512,1024]{2,1,0:T(8,128)(2,1)} %get-tuple-element.7, s32[1024]{0:T(1024)S(1)} %pad_clamp_fusion), kind=kCustom, calls=%fused_computation | custom fusion | bytes 8388624 | tf_op jit(solution)/shard_map/jit(_take)/gather | solution.py:91
  262.4 5.0 %gather_fusion.1 = bf16[4,512,1024]{2,1,0:T(8,128)(2,1)} fusion(bf16[4,512,1024]{2,1,0:T(8,128)(2,1)} %get-tuple-element.8, s32[1024]{0:T(1024)S(1)} %pad_clamp_fusion), kind=kCustom, calls=%fused_computation.1 | custom fusion | bytes 8388624 | tf_op jit(solution)/shard_map/jit(_take)/gather | solution.py:91
  267.4 42.7 %all-to-all-done.2 = bf16[2,32,128,256]{3,2,0,1:T(8,128)(2,1)} async-done(((bf16[2,32,128,256]{3,2,0,1:T(8,128)(2,1)}), bf16[2,32,128,256]{3,2,0,1:T(8,128)(2,1)}, u32[]{:S(2)}, u32[]{:S(2)}) %all-to-all-start.2) | async-done | bytes 4194336 | tf_op jit(solution)/shard_map/all_to_all | solution.py:96
  310.1 7.5 %copy.24 = bf16[2,4,8,128,256]{3,2,4,0,1:T(8,128)(2,1)} copy(bf16[2,4,8,128,256]{4,3,0,1,2:T(8,128)(2,1)} %bitcast.26) | data formatting | bytes 8388608 | tf_op jit(solution)/shard_map/all_to_all | solution.py:96
  317.6 7.3 %all_to_all.47 = bf16[2,4,1024,256]{2,3,0,1:T(8,128)(2,1)} reshape(bf16[2,4,8,128,256]{3,2,4,0,1:T(8,128)(2,1)} %copy.24) | data formatting | bytes 8388608 | tf_op jit(solution)/shard_map/all_to_all | solution.py:96
  324.9 11.2 %convert_bitcast_fusion = bf16[2,4,1024,256]{2,3,0,1:T(8,128)(2,1)} fusion(bf16[2,4,1024,256]{2,3,0,1:T(8,128)(2,1)} %all_to_all.47, bf16[4,512,1024]{2,1,0:T(8,128)(2,1)} %gather_fusion.1, bf16[4,512,1024]{2,1,0:T(8,128)(2,1)} %gather_fusion, pred[4]{0:T(512)(128)(4,1)S(1)} %and_bitcast_fusion), kind=kOutput, calls=%fused_computation.19 | convolution fusion | flops 4318035968 | bytes 16777220 | tf_op jit(solution)/shard_map/bgf,cbfm->cbgm/dot_general | solution.py:93
  336.1 6.2 %copy.25 = bf16[2,4,1024,256]{3,2,1,0:T(8,128)(2,1)} copy(bf16[2,4,1024,256]{2,3,0,1:T(8,128)(2,1)} %convert_bitcast_fusion) | data formatting | bytes 8388608 | tf_op jit(solution)/shard_map/convert_element_type | solution.py:98
  (16 shorter events, 4.9 us)
Async XLA Ops:
  1.3 6.4 %collective-permute-start = (f32[128,16]{1,0:T(8,128)S(1)}, f32[128,16]{1,0:T(8,128)S(1)}, u32[]{:S(2)}, u32[]{:S(2)}) collective-permute-start(f32[128,16]{1,0:T(8,128)S(1)} %get-tuple-element.11), channel_id=1, source_target_pairs={{0,8},{8,16},{16,24},{24,32},{32,40},{40,48},{48,56},{56,64},{64,7... | collective-permute-start | bytes 24584 | tf_op jit(solution)/shard_map/ppermute | solution.py:18
  6.3 5.2 %collective-permute-start.1 = (f32[128,16]{1,0:T(8,128)S(1)}, f32[128,16]{1,0:T(8,128)S(1)}, u32[]{:S(2)}, u32[]{:S(2)}) collective-permute-start(f32[128,16]{1,0:T(8,128)S(1)} %get-tuple-element.12), channel_id=1, source_target_pairs={{8,0},{16,8},{24,16},{32,24},{40,32},{48,40},{56,48},{64,56},{72,6... | collective-permute-start | bytes 24584 | tf_op jit(solution)/shard_map/ppermute | solution.py:19
  20.3 58.2 %all-to-all-start = ((bf16[2,32,128,256]{3,1,0,2:T(8,128)(2,1)}), bf16[2,32,128,256]{3,1,0,2:T(8,128)(2,1)}, u32[]{:S(2)}, u32[]{:S(2)}) async-start(bf16[2,32,128,256]{3,1,0,2:T(8,128)(2,1)} %multiply_convert_fusion), calls=%async_computation | async-start | bytes 8388608 | tf_op jit(solution)/shard_map/all_to_all | solution.py:89
  246.1 5.4 %copy-start = (s32[4,1]{0,1:T(1,128)S(1)}, s32[4,1]{0,1:T(1,128)}, u32[]{:S(2)}) copy-start(s32[4,1]{0,1:T(1,128)} %param.12) | copy-start | bytes 52
  246.1 64.1 %all-to-all-start.2 = ((bf16[2,32,128,256]{3,2,0,1:T(8,128)(2,1)}), bf16[2,32,128,256]{3,2,0,1:T(8,128)(2,1)}, u32[]{:S(2)}, u32[]{:S(2)}) async-start(bf16[2,32,128,256]{3,2,0,1:T(8,128)(2,1)} %bitcast.76), calls=%async_computation.2 | async-start | bytes 8388608 | tf_op jit(solution)/shard_map/all_to_all | solution.py:96
where the time goes:
time: 345 us; the launch traced here: 342 us
  local copies, waits for them, and re-layouts  116 us (34%)
  waiting for transfers between devices  98.3 us (28%)
  blocking collectives  63.5 us (18%)
  matrix products  32.1 us (9%)
  other arithmetic  16 us (5%)
  starting transfers between devices  16 us (5%)
    all_to_all x1, blocking collectives, shards(): lax.all_to_all(spectrum, 'tm', split_axis=3, concat_axis=2, tiled=True)  63.5 us
    all_to_all x1, waiting for transfers between devices, shards(): lax.all_to_all(weighted, 'tm', split_axis=2, concat_axis=3, tiled=True)  50.4 us
    all_to_all x1, waiting for transfers between devices, shards(): lax.all_to_all(moved, 'freq', split_axis=1, concat_axis=2, tiled=True)  42.7 us
    unnamed x4, local copies, waits for them, and re-layouts  36.8 us
    convert_element_type x1, local copies, waits for them, and re-layouts, sidereal_transform(): return finished.astype(jnp.bfloat16)  23.2 us
    all_to_all x1, local copies, waits for them, and re-layouts, shards(): lax.all_to_all(spectrum, 'tm', split_axis=3, concat_axis=2, tiled=True)  19.5 us
    gather x3, local copies, waits for them, and re-layouts, shards(): chosen = jnp.take(filter_bank, baseline_delay_class[:, 0], axis=0)  15.8 us
    all_to_all x2, local copies, waits for them, and re-layouts, shards(): lax.all_to_all(moved, 'freq', split_axis=1, concat_axis=2, tiled=True)  14.8 us
  transfers between devices with their start and end apart: 4, of which 4 were waited for; matrix products, arithmetic and copies ran while one was open for 5% of the time, Pallas kernels for 0%

commit v1 on v0

v1 whole, which is shorter than its diff:
```python
import functools
import math
import random

import jax
import jax.numpy as jnp
import numpy as np
from jax import lax
from jax.experimental import pallas as pl
from jax.experimental.pallas import tpu as pltpu
from jax.sharding import PartitionSpec as P

RIM = 16
MESH = pl.DeviceIdType.MESH
TM, FREQ = 16, 8
CHAN, LEN = 128, 256
SAMPLES = TM * LEN
BLOCK = 4
BF, F32 = jnp.bfloat16, jnp.float32
OFFSETS = [(a, b, c) for a in range(4) for b in range(2) for c in range(2)]


def shuffled(seed):
    order = list(OFFSETS)
    random.Random(seed).shuffle(order)
    return order


def dft_tables():
    k = np.arange(LEN)
    angle = 2.0 * np.pi / LEN * (k[:, None] * k[None, :] % LEN)
    c, s = np.cos(angle), np.sin(angle)
    full = np.block([[c, s], [-s, c]]).astype(np.float32)
    high = full.astype(jnp.bfloat16)
    low = (full - high.astype(np.float32)).astype(jnp.bfloat16)
    turn = 2.0 * np.pi / SAMPLES * (np.arange(TM)[:, None] * k[None, :])
    twist = np.stack([np.cos(turn), np.sin(turn)]) / math.sqrt(SAMPLES)
    return high, low, twist.astype(np.float32)


def order_table():
    m = np.arange(LEN)
    table = np.zeros((LEN, LEN), np.float32)
    table[m, (m % TM) * TM + m // TM] = 1.0
    return table.astype(jnp.bfloat16)


def place(i, j):
    return i // 4, lax.rem(i // 2, 2), lax.rem(i, 2), j // 2, lax.rem(j, 2)


def tm_index(x, zh, core, o):
    return lax.rem(x + o[0], 4) * 4 + lax.rem(zh + o[1], 2) * 2 + lax.rem(core + o[2], 2)


def owner_block(x, core, y, zl, e):
    return lax.rem(y + 2 * core + lax.rem(e + x, 2), 4) * 2 + lax.rem(zl + e, 2)


def cmul_w16(r, i, n):
    n %= 16
    if n == 0:
        return r, i
    if n == 4:
        return i, -r
    if n == 8:
        return -r, -i
    if n == 12:
        return -i, r
    if n == 2:
        h = math.sqrt(0.5)
        return (r + i) * h, (i - r) * h
    if n == 6:
        h = math.sqrt(0.5)
        return (i - r) * h, -(r + i) * h
    c, s = math.cos(2 * math.pi * n / 16), math.sin(2 * math.pi * n / 16)
    return r * c + i * s, i * c - r * s


def radix4(v):
    (ar, ai), (br, bi), (cr, ci), (dr, di) = v
    pr, pi = ar + cr, ai + ci
    qr, qi = ar - cr, ai - ci
    sr, si = br + dr, bi + di
    tr, ti = br - dr, bi - di
    return [(pr + sr, pi + si), (qr + ti, qi - tr), (pr - sr, pi - si), (qr - ti, qi + tr)]


def exchange_kernel(
    vis_hbm, power_ref, square_ref, count_ref, mask_ref, high_ref, low_ref, twist_ref,
    out_ref,
    vis, pad, smooth, recv, yhigh, ylow, send,
    vis_sem, halo_send, halo_recv, send1, recv1, send2, recv2,
):
    i, j = lax.axis_index("tm"), lax.axis_index("freq")
    x, zh, core, y, zl = place(i, j)
    barrier = pltpu.get_barrier_semaphore()

    def greet(k, _):
        n = lax.rem(i * FREQ + j + k, TM * FREQ)
        pl.semaphore_signal(barrier, inc=1, device_id=(n // FREQ, lax.rem(n, FREQ)), device_id_type=MESH)
        return 0

    lax.fori_loop(1, TM * FREQ, greet, 0)
    load = pltpu.make_async_copy(vis_hbm, vis, vis_sem)
    load.start()

    counts = count_ref[...].astype(F32)
    power = power_ref[...]
    kurtosis = (counts + 1.0) / (counts - 1.0) * (counts * square_ref[...] / (power * power) - 1.0)
    pad[:, 128:384] = mask_ref[...].astype(F32) * jnp.exp(-2.0 * (kurtosis - 1.0) ** 2)

    pl.semaphore_wait(barrier, TM * FREQ - 1)
    right, left = lax.rem(i + 1, TM), lax.rem(i + TM - 1, TM)
    to_right = pltpu.make_async_remote_copy(
        pad.at[:, 256:384], pad.at[:, 0:128], halo_send.at[0], halo_recv.at[0],
        device_id=(right, j), device_id_type=MESH)
    to_left = pltpu.make_async_remote_copy(
        pad.at[:, 128:256], pad.at[:, 384:512], halo_send.at[1], halo_recv.at[1],
        device_id=(left, j), device_id_type=MESH)
    to_right.start()
    to_left.start()
    to_right.wait()
    to_left.wait()

    width = 512
    for rows in range(0, CHAN, 32):
        base = pad[rows : rows + 32, :]
        for direction in (0, 1):
            def shift(v, n):
                return pltpu.roll(v, n if direction else width - n, 1)
            total = base
            for n in (1, 2, 4, 8):
                total = total + shift(total, n)
            base = total + shift(base, 16)
        smooth[rows : rows + 32, :] = base[:, 128:384] * (1.0 / (RIM + 1) ** 2)

    load.wait()

    def weigh(e, o):
        d = tm_index(x, zh, core, o)
        dx, dzh, dcore, _, _ = place(d, j)
        b = BLOCK * owner_block(dx, dcore, y, zl, e) + 2 * (dx // 2) + dzh
        for c in range(2):
            vis[c, b] = (vis[c, b].astype(F32) * smooth[...]).astype(BF)
            if o == (0, 0, 0):
                pltpu.make_async_copy(vis.at[c, b], recv.at[e, i, c], recv1.at[e]).start()
            else:
                pltpu.make_async_remote_copy(
                    vis.at[c, b], recv.at[e, i, c], send1.at[e], recv1.at[e],
                    device_id=(d, j), device_id_type=MESH).start()

    for e in range(2):
        for o in shuffled(11 + e):
            weigh(e, o)

    for e in range(2):
        pltpu.make_async_copy(recv.at[e], recv.at[e], recv1.at[e]).wait()

        def combine(step, _):
            rows = pl.ds(pl.multiple_of((step // 2) * 16, 16), 16)
            col = pl.multiple_of(lax.rem(step, 2) * 128, 128)
            cols = pl.ds(col, 128)
            inner = []
            for b in range(4):
                part = []
                for a in range(4):
                    p = 4 * a + b
                    part.append((recv[e, p, 0, rows, cols].astype(F32), recv[e, p, 1, rows, cols].astype(F32)))
                part = radix4(part)
                inner.append([cmul_w16(*part[c], b * c) for c in range(4)])
            for c in range(4):
                outer = radix4([inner[b][c] for b in range(4)])
                for d in range(4):
                    q = c + 4 * d
                    r, m = outer[d]
                    cosine = twist_ref[0, q : q + 1, cols]
                    sine = twist_ref[1, q : q + 1, cols]
                    for part, value in ((0, r * cosine + m * sine), (1, m * cosine - r * sine)):
                        top = value.astype(BF)
                        at = (q, rows, pl.ds(pl.multiple_of(col + LEN * part, 128), 128))
                        yhigh[at] = top
                        ylow[at] = (value - top.astype(F32)).astype(BF)
            return 0

        lax.fori_loop(0, 2 * CHAN // 16, combine, 0)

        dims = (((1,), (1,)), ((), ()))

        def transform(step, _):
            q = 2 * step
            yh = yhigh[pl.ds(q, 2)].reshape(2 * CHAN, 2 * LEN)
            yl = ylow[pl.ds(q, 2)].reshape(2 * CHAN, 2 * LEN)
            for part in range(2):
                rows = slice(LEN * part, LEN * part + LEN)
                value = lax.dot_general(high_ref[rows], yh, dims, preferred_element_type=F32)
                value += lax.dot_general(high_ref[rows], yl, dims, preferred_element_type=F32)
                value += lax.dot_general(low_ref[rows], yh, dims, preferred_element_type=F32)
                value = value.astype(BF)
                for h in range(2):
                    at = pl.ds(pl.multiple_of((q + h) * 16, 16), 16)
                    send[e, part, :, at, :] = value[:, CHAN * h : CHAN * h + CHAN].reshape(TM, TM, CHAN)
            return 0

        lax.fori_loop(0, TM // 2, transform, 0)

        dest = owner_block(x, core, y, zl, e)
        slot = 2 * (x // 2) + zh
        lanes = pl.ds(pl.multiple_of(j * CHAN, CHAN), CHAN)
        for o in shuffled(21 + e):
            d = tm_index(x, zh, core, o)
            for c in range(2):
                def away():
                    pltpu.make_async_remote_copy(
                        send.at[e, c, d], out_ref.at[slot, c, :, lanes], send2, recv2,
                        device_id=(d, dest), device_id_type=MESH).start()
                if o != (0, 0, 0) or e == 1:
                    away()
                else:
                    pl.when(dest != j)(away)

                    @pl.when(dest == j)
                    def _():
                        pltpu.make_async_copy(send.at[e, c, d], out_ref.at[slot, c, :, lanes], recv2).start()

    pltpu.make_async_copy(out_ref, out_ref, recv2).wait()
    for e in range(2):
        pltpu.make_async_copy(recv.at[e, pl.ds(0, TM - 1)], recv.at[e, pl.ds(0, TM - 1)], send1.at[e]).wait()
    own = owner_block(x, core, y, zl, 0) == j

    @pl.when(own)
    def _():
        whole = vis.at[:, pl.ds(0, 31)]
        pltpu.make_async_copy(whole, whole, send2).wait()

    @pl.when(jnp.logical_not(own))
    def _():
        pltpu.make_async_copy(vis, vis, send2).wait()


def exchange(vis, power, square, count, mask):
    high, low, twist = dft_tables()
    vmem, hbm = pl.BlockSpec(memory_space=pltpu.VMEM), pl.BlockSpec(memory_space=pl.ANY)
    dma = pltpu.SemaphoreType.DMA
    return pl.pallas_call(
        exchange_kernel,
        name="exchange",
        out_shape=jax.ShapeDtypeStruct((BLOCK, 2, LEN, FREQ * CHAN), BF),
        in_specs=[hbm] + [vmem] * 7,
        out_specs=hbm,
        scratch_shapes=[
            pltpu.VMEM((2, BLOCK * FREQ, CHAN, LEN), BF),
            pltpu.VMEM((CHAN, 512), F32),
            pltpu.VMEM((CHAN, LEN), F32),
            pltpu.VMEM((2, TM, 2, CHAN, LEN), BF),
            pltpu.VMEM((TM, CHAN, 2 * LEN), BF),
            pltpu.VMEM((TM, CHAN, 2 * LEN), BF),
            pltpu.VMEM((2, 2, TM, LEN, CHAN), BF),
            dma, dma((2,)), dma((2,)), dma((2,)), dma((2,)), dma, dma,
        ],
        compiler_params=pltpu.CompilerParams(
            collective_id=0, has_side_effects=True, vmem_limit_bytes=56 << 20),
    )(vis, power, square, count, mask, jnp.asarray(high), jnp.asarray(low), jnp.asarray(twist))


def filter_kernel(class_ref, spec_ref, order_ref, bank_ref, out_ref, held):
    @pl.when(pl.program_id(1) == 0)
    def _():
        for c in range(2):
            held[LEN * c : LEN * c + LEN, :] = jnp.dot(
                order_ref[...], spec_ref[0, c], preferred_element_type=F32).astype(BF)

    value = lax.dot_general(
        bank_ref[0], held[...], (((1,), (1,)), ((), ())), preferred_element_type=F32).astype(BF)
    for c in range(2):
        out_ref[c, 0] = value[:, LEN * c : LEN * c + LEN]


def delay_filter(spectrum, classes, bank):
    width = FREQ * CHAN
    tile = 512
    return pl.pallas_call(
        filter_kernel,
        name="delay_filter",
        out_shape=jax.ShapeDtypeStruct((2, BLOCK, width, LEN), BF),
        grid_spec=pltpu.PrefetchScalarGridSpec(
            num_scalar_prefetch=1,
            grid=(BLOCK, width // tile),
            in_specs=[
                pl.BlockSpec((1, 2, LEN, width), lambda b, g, cls: (b, 0, 0, 0)),
                pl.BlockSpec((LEN, LEN), lambda b, g, cls: (0, 0)),
                pl.BlockSpec((1, tile, width), lambda b, g, cls: (cls[b], g, 0)),
            ],
            out_specs=pl.BlockSpec((2, 1, tile, LEN), lambda b, g, cls: (0, b, g, 0)),
            scratch_shapes=[pltpu.VMEM((2 * LEN, width), BF)],
        ),
        compiler_params=pltpu.CompilerParams(vmem_limit_bytes=40 << 20),
    )(classes, spectrum, jnp.asarray(order_table()), bank)


def shards(visibility, power, square, count, mask, classes, bank):
    spectrum = exchange(visibility, power, square, count, mask)
    return delay_filter(spectrum, classes[:, 0], bank)


def solution(mesh):
    in_specs = (
        P(None, None, "freq", "tm"),
        P("freq", "tm"),
        P("freq", "tm"),
        P("freq", "tm"),
        P("freq", "tm"),
        P("freq", None),
        P(),
    )
    out_specs = P(None, "freq", None, "tm")
    return jax.shard_map(shards, mesh=mesh, in_specs=in_specs, out_specs=out_specs, check_vma=False)
```

time: 345 us -> 140 us (0.41)
  Pallas kernels: 0 us -> 134 us
  local copies, waits for them, and re-layouts: 116 us -> 5.57 us
  waiting for transfers between devices: 98.3 us -> 0 us
  blocking collectives: 63.5 us -> 0 us
  matrix products: 32.1 us -> 0 us
  other arithmetic: 16 us -> 0 us
  starting transfers between devices: 16 us -> 0 us
    pallas_call x0 -> x2, Pallas kernels: none -> 134 us  [the longest x1 125 us: exchange(): pl.pallas_call(exchange_kernel, name='exchange', out_shape=jax.ShapeDtype...]
    all_to_all x2 -> x0, waiting for transfers between devices: 93.1 us -> none  [the longest x1 50.4 us: shards(): lax.all_to_all(weighted, 'tm', split_axis=2, concat_axis=3, tiled=True)]
    all_to_all x1 -> x0, blocking collectives: 63.5 us -> none  [shards(): lax.all_to_all(spectrum, 'tm', split_axis=3, concat_axis=2, tiled=True)]
    all_to_all x3 -> x0, local copies, waits for them, and re-layouts: 34.3 us -> none  [the longest x1 19.5 us: shards(): lax.all_to_all(spectrum, 'tm', split_axis=3, concat_axis=2, tiled=True)]
    dot_general x3 -> x0, matrix products: 32.1 us -> none  [the longest x1 11.2 us: shards(): jnp.einsum('bgf,cbfm->cbgm', chosen, lax.all_to_all(moved, 'freq', split_...]
    unnamed x4 -> x8, local copies, waits for them, and re-layouts: 36.8 us -> 5.57 us
    convert_element_type x2 -> x0, local copies, waits for them, and re-layouts: 29.4 us -> none  [the longest x1 23.2 us: sidereal_transform(): return finished.astype(jnp.bfloat16)]
    gather x3 -> x0, local copies, waits for them, and re-layouts: 15.8 us -> none  [shards(): chosen = jnp.take(filter_bank, baseline_delay_class[:, 0], axis=0)]
  transfers between devices with their start and end apart: 4 -> 0, of which waited for: 4 -> 0; matrix products, arithmetic and copies ran while one was open for 5% -> 0% of each run, Pallas kernels for 0% -> 0%
where the time goes in v1:
time: 140 us
  Pallas kernels  134 us (96%)
  local copies, waits for them, and re-layouts  5.57 us (4%)
    pallas_call x1, Pallas kernels, exchange(): pl.pallas_call(exchange_kernel, name='exchange', out_shape=jax.ShapeDtype...  125 us
    pallas_call x1, Pallas kernels, delay_filter(): pl.pallas_call(filter_kernel, name='delay_filter', out_shape=jax.ShapeDty...  9.29 us
    unnamed x8, local copies, waits for them, and re-layouts  5.57 us

profile of v1, /device:TPU:1, one launch (start us, length us, event | category | flops | bytes accessed | tf_op | source)
XLA Modules:
  0.0 139.7 jit_solution(15265707827351532580)
XLA Ops:
  0.0 0.0 copy-start.2
  0.0 0.0 copy-start.3
  0.0 124.8 %exchange.1.spec_ref = bf16[4,2,256,1024]{3,2,1,0:T(8,128)(2,1)} custom-call(bf16[2,32,128,256]{3,2,1,0:T(8,128)(2,1)} %vis_hbm.1, f32[128,256]{1,0:T(8,128)} %power_ref.1, f32[128,256]{1,0:T(8,128)} %square_ref.1, s32[128,256]{1,0:T(8,128)} %count_ref.1, s32[128,256]{1,0:T(8,128)} %mask_ref.1, bf16[512,512]{1,0:T(8,128)(2,1)} %constant.8.clone.high_ref, ...), custom_call_target="tpu_custom_call" | custom-call | tf_op jit(solution)/shard_map/exchange/pallas_call | solution.py:245
  124.8 0.0 copy-done.2
  124.8 0.0 copy-done.3
  124.8 0.0 copy-start
  124.8 2.2 %copy-done = bf16[4,2,256,1024]{3,2,1,0:T(8,128)(2,1)S(1)} copy-done((bf16[4,2,256,1024]{3,2,1,0:T(8,128)(2,1)S(1)}, bf16[4,2,256,1024]{3,2,1,0:T(8,128)(2,1)}, u32[]{:S(2)}) %copy-start) | copy-done | bytes 4194328
  127.0 0.0 copy-start.1
  127.0 3.4 %copy-done.1 = bf16[4,1024,1024]{2,1,0:T(8,128)(2,1)S(1)} copy-done((bf16[4,1024,1024]{2,1,0:T(8,128)(2,1)S(1)}, bf16[4,1024,1024]{2,1,0:T(8,128)(2,1)}, u32[]{:S(2)}) %copy-start.1) | copy-done | bytes 8388632
  130.4 9.3 %delay_filter.1 = bf16[2,4,1024,256]{3,2,1,0:T(8,128)(2,1)} custom-call(s32[4]{0:T(128)S(1)} %bitcast.1, bf16[4,2,256,1024]{3,2,1,0:T(8,128)(2,1)S(1)} %copy-done, bf16[256,256]{1,0:T(8,128)(2,1)S(1)} %copy-done.2, bf16[4,1024,1024]{2,1,0:T(8,128)(2,1)S(1)} %copy-done.1), custom_call_target="tpu_custom_call" | custom-call | tf_op jit(solution)/shard_map/delay_filter/pallas_call | solution.py:282
Async XLA Ops:
  0.0 124.8 %copy-start.2 = (bf16[256,256]{1,0:T(8,128)(2,1)S(1)}, bf16[256,256]{1,0:T(8,128)(2,1)}, u32[]{:S(2)}) copy-start(bf16[256,256]{1,0:T(8,128)(2,1)} %constant.11.clone.order_ref) | copy-start | bytes 393220
  0.0 124.8 %copy-start.3 = (s32[4,1]{0,1:T(1,128)S(1)}, s32[4,1]{0,1:T(1,128)}, u32[]{:S(2)}) copy-start(s32[4,1]{0,1:T(1,128)} %param.16) | copy-start | bytes 52
  124.8 2.2 %copy-start = (bf16[4,2,256,1024]{3,2,1,0:T(8,128)(2,1)S(1)}, bf16[4,2,256,1024]{3,2,1,0:T(8,128)(2,1)}, u32[]{:S(2)}) copy-start(bf16[4,2,256,1024]{3,2,1,0:T(8,128)(2,1)} %exchange.1.spec_ref) | copy-start | bytes 12582916
  127.0 3.4 %copy-start.1 = (bf16[4,1024,1024]{2,1,0:T(8,128)(2,1)S(1)}, bf16[4,1024,1024]{2,1,0:T(8,128)(2,1)}, u32[]{:S(2)}) copy-start(bf16[4,1024,1024]{2,1,0:T(8,128)(2,1)} %bank_ref.1) | copy-start | bytes 25165828

commit v2 on v1

v2 whole, which is shorter than its diff:
```python
import functools
import math
import random

import jax
import jax.numpy as jnp
import numpy as np
from jax import lax
from jax.experimental import pallas as pl
from jax.experimental.pallas import tpu as pltpu
from jax.sharding import PartitionSpec as P

RIM = 16
MESH = pl.DeviceIdType.MESH
TM, FREQ = 16, 8
CHAN, LEN = 128, 256
SAMPLES = TM * LEN
BLOCK = 4
BF, F32 = jnp.bfloat16, jnp.float32
PIECES_1, PIECES_2 = 4, 4
ORDER_1, ORDER_2 = 11, 21
OFFSETS = [(a, b, c) for a in range(4) for b in range(2) for c in range(2)]


def shuffled(seed):
    order = list(OFFSETS)
    random.Random(seed).shuffle(order)
    return order


def dft_tables():
    k = np.arange(LEN)
    angle = 2.0 * np.pi / LEN * (k[:, None] * k[None, :] % LEN)
    c, s = np.cos(angle), np.sin(angle)
    full = np.block([[c, s], [-s, c]]).astype(np.float32)
    high = full.astype(jnp.bfloat16)
    low = (full - high.astype(np.float32)).astype(jnp.bfloat16)
    turn = 2.0 * np.pi / SAMPLES * (np.arange(TM)[:, None] * k[None, :])
    twist = np.stack([np.cos(turn), np.sin(turn)]) / math.sqrt(SAMPLES)
    return high, low, twist.astype(np.float32)


def order_table():
    m = np.arange(LEN)
    table = np.zeros((LEN, LEN), np.float32)
    table[m, (m % TM) * TM + m // TM] = 1.0
    return table.astype(jnp.bfloat16)


def place(i, j):
    return i // 4, lax.rem(i // 2, 2), lax.rem(i, 2), j // 2, lax.rem(j, 2)


def tm_index(x, zh, core, o):
    return lax.rem(x + o[0], 4) * 4 + lax.rem(zh + o[1], 2) * 2 + lax.rem(core + o[2], 2)


def owner_block(x, core, y, zl, e):
    return lax.rem(y + 2 * core + lax.rem(e + x, 2), 4) * 2 + lax.rem(zl + x // 2, 2)


def cmul_w16(r, i, n):
    n %= 16
    if n == 0:
        return r, i
    if n == 4:
        return i, -r
    if n == 8:
        return -r, -i
    if n == 12:
        return -i, r
    if n == 2:
        h = math.sqrt(0.5)
        return (r + i) * h, (i - r) * h
    if n == 6:
        h = math.sqrt(0.5)
        return (i - r) * h, -(r + i) * h
    c, s = math.cos(2 * math.pi * n / 16), math.sin(2 * math.pi * n / 16)
    return r * c + i * s, i * c - r * s


def radix4(v):
    (ar, ai), (br, bi), (cr, ci), (dr, di) = v
    pr, pi = ar + cr, ai + ci
    qr, qi = ar - cr, ai - ci
    sr, si = br + dr, bi + di
    tr, ti = br - dr, bi - di
    return [(pr + sr, pi + si), (qr + ti, qi - tr), (pr - sr, pi - si), (qr - ti, qi + tr)]


def box(v, direction):
    width = v.shape[1]

    def shift(u, n):
        return pltpu.roll(u, n if direction else width - n, 1)

    total = v
    for n in (1, 2, 4, 8):
        total = total + shift(total, n)
    return total + shift(v, 16)


def triangle(v):
    return box(box(v, 0), 1) * (1.0 / (RIM + 1) ** 2)


def exchange_kernel(
    class_ref, vis_hbm, power_ref, square_ref, count_ref, mask_ref, high_ref, low_ref, twist_ref, order_ref, bank_hbm,
    last_ref, real_ref, imag_ref,
    vis, flags, edge, smooth, recv, yhigh, ylow, send, spec, bank, held, done,
    load_sem, halo_send, halo_recv, send1, recv1, send2, recv2, done_sem,
):
    i, j = lax.axis_index("tm"), lax.axis_index("freq")
    x, zh, core, y, zl = place(i, j)
    barrier = pltpu.get_barrier_semaphore()

    for k in range(1, TM):
        pl.semaphore_signal(barrier, inc=1, device_id=(lax.rem(i + k, TM), j), device_id_type=MESH)
    for k in range(1, FREQ):
        pl.semaphore_signal(barrier, inc=1, device_id=(i, lax.rem(j + k, FREQ)), device_id_type=MESH)
    load = pltpu.make_async_copy(vis_hbm, vis, load_sem.at[0])
    load.start()

    counts = count_ref[...].astype(F32)
    power = power_ref[...]
    kurtosis = (counts + 1.0) / (counts - 1.0) * (counts * square_ref[...] / (power * power) - 1.0)
    flags[...] = mask_ref[...].astype(F32) * jnp.exp(-2.0 * (kurtosis - 1.0) ** 2)

    pl.semaphore_wait(barrier, TM + FREQ - 2)
    right, left = lax.rem(i + 1, TM), lax.rem(i + TM - 1, TM)
    to_right = pltpu.make_async_remote_copy(
        flags.at[:, LEN - 128 : LEN], edge.at[0], halo_send.at[0], halo_recv.at[0],
        device_id=(right, j), device_id_type=MESH)
    to_left = pltpu.make_async_remote_copy(
        flags.at[:, 0:128], edge.at[1], halo_send.at[1], halo_recv.at[1],
        device_id=(left, j), device_id_type=MESH)
    to_right.start()
    to_left.start()
    blank = jnp.zeros((32, 128), F32)
    for rows in range(0, CHAN, 32):
        own = jnp.concatenate([blank, flags[rows : rows + 32, :], blank], axis=1)
        smooth[rows : rows + 32, :] = triangle(own)[:, 128 : 128 + LEN]
    to_right.wait()
    to_left.wait()
    lane = lax.broadcasted_iota(jnp.int32, (CHAN, 128), 1)
    first_lanes, last_lanes = lane < RIM, lane >= 128 - RIM
    before = triangle(jnp.where(last_lanes, edge[0], 0.0))
    after = triangle(jnp.where(first_lanes, edge[1], 0.0))
    smooth[:, 0:128] += jnp.where(first_lanes, before, 0.0)
    smooth[:, LEN - 128 : LEN] += jnp.where(last_lanes, after, 0.0)

    load.wait()
    bank_load = pltpu.make_async_copy(bank_hbm, bank, load_sem.at[1])
    bank_load.start()

    def first(e, o):
        d = tm_index(x, zh, core, o)
        dx, dzh, dcore, _, _ = place(d, j)
        return d, BLOCK * owner_block(dx, dcore, y, zl, e) + 2 * e + dzh

    def weigh(e, o):
        d, b = first(e, o)
        for c in range(2):
            value = (vis[c, b].astype(F32) * smooth[...]).astype(BF)
            if o == (0, 0, 0):
                recv[e, i, c] = value
            else:
                vis[c, b] = value

    def hand(e, o, c, rows):
        d, b = first(e, o)
        pltpu.make_async_remote_copy(
            vis.at[c, b, rows], recv.at[e, i, c, rows], send1.at[e], recv1.at[e],
            device_id=(d, j), device_id_type=MESH).start()

    size = CHAN // PIECES_1
    for e in range(2):
        order = shuffled(ORDER_1 + e)
        remote = [o for o in order if o != (0, 0, 0)]
        for o in order:
            weigh(e, o)
            if o != (0, 0, 0):
                hand(e, o, 0, pl.ds(0, size))
        def rest(q, _):
            rows = pl.ds(pl.multiple_of(q * size, size), size)
            for o in remote:
                hand(e, o, 0, rows)
            return 0
        lax.fori_loop(1, PIECES_1, rest, 0)
        def rest(q, _):
            rows = pl.ds(pl.multiple_of(q * size, size), size)
            for o in remote:
                hand(e, o, 1, rows)
            return 0
        lax.fori_loop(0, PIECES_1, rest, 0)

    for e in range(2):
        others = recv.at[e, pl.ds(0, TM - 1)]
        pltpu.make_async_copy(others, others, recv1.at[e]).wait()

        def combine(step, _):
            rows = pl.ds(pl.multiple_of((step // 2) * 16, 16), 16)
            col = pl.multiple_of(lax.rem(step, 2) * 128, 128)
            cols = pl.ds(col, 128)
            inner = []
            for b in range(4):
                part = []
                for a in range(4):
                    p = 4 * a + b
                    part.append((recv[e, p, 0, rows, cols].astype(F32), recv[e, p, 1, rows, cols].astype(F32)))
                part = radix4(part)
                inner.append([cmul_w16(*part[c], b * c) for c in range(4)])
            for c in range(4):
                outer = radix4([inner[b][c] for b in range(4)])
                for d in range(4):
                    q = c + 4 * d
                    r, m = outer[d]
                    cosine = twist_ref[0, q : q + 1, cols]
                    sine = twist_ref[1, q : q + 1, cols]
                    for part, value in ((0, r * cosine + m * sine), (1, m * cosine - r * sine)):
                        top = value.astype(BF)
                        at = (q, rows, pl.ds(pl.multiple_of(col + LEN * part, 128), 128))
                        yhigh[at] = top
                        ylow[at] = (value - top.astype(F32)).astype(BF)
            return 0

        lax.fori_loop(0, 2 * CHAN // 16, combine, 0)

        dims = (((1,), (1,)), ((), ()))

        def transform(step, _):
            q = 2 * step
            yh = yhigh[pl.ds(q, 2)].reshape(2 * CHAN, 2 * LEN)
            yl = ylow[pl.ds(q, 2)].reshape(2 * CHAN, 2 * LEN)
            for part in range(2):
                rows = slice(LEN * part, LEN * part + LEN)
                value = lax.dot_general(high_ref[rows], yh, dims, preferred_element_type=F32)
                value += lax.dot_general(high_ref[rows], yl, dims, preferred_element_type=F32)
                value += lax.dot_general(low_ref[rows], yh, dims, preferred_element_type=F32)
                value = value.astype(BF)
                for h in range(2):
                    at = pl.ds(pl.multiple_of((q + h) * 16, 16), 16)
                    send[e, part, :, at, :] = value[:, CHAN * h : CHAN * h + CHAN].reshape(TM, TM, CHAN)
            return 0

        lax.fori_loop(0, TM // 2, transform, 0)

        dest = owner_block(x, core, y, zl, e)
        lanes = pl.ds(pl.multiple_of(j * CHAN, CHAN), CHAN)
        size2 = LEN // PIECES_2
        for c in range(2):
            part = 2 * e + c
            target = last_ref if part == 3 else spec.at[part]

            def share(q, _):
                rows = pl.ds(pl.multiple_of(q * size2, size2), size2)
                for o in shuffled(ORDER_2 + e):
                    d = tm_index(x, zh, core, o)

                    def away():
                        pltpu.make_async_remote_copy(
                            send.at[e, c, d, rows], target.at[zh, rows, lanes], send2, recv2.at[part],
                            device_id=(d, dest), device_id_type=MESH).start()

                    if o != (0, 0, 0):
                        away()
                    else:
                        pl.when(dest != j)(away)

                        @pl.when(dest == j)
                        def _():
                            pltpu.make_async_copy(
                                send.at[e, c, d, rows], target.at[zh, rows, lanes], recv2.at[part]).start()
                return 0

            lax.fori_loop(0, PIECES_2, share, 0)

    bank_load.wait()
    out = []
    for part in range(3):
        e, c = part // 2, part % 2
        pltpu.make_async_copy(spec.at[part], spec.at[part], recv2.at[part]).wait()
        for z in range(2):
            held[...] = jnp.dot(order_ref[...], spec[part, z], preferred_element_type=F32).astype(BF)

            def rows_of(g, _):
                at = pl.ds(pl.multiple_of(g * 512, 512), 512)
                done[part, z, at, :] = lax.dot_general(
                    bank[class_ref[2 * e + z], at, :], held[...], (((1,), (1,)), ((), ())),
                    preferred_element_type=F32).astype(BF)
                return 0

            lax.fori_loop(0, 2, rows_of, 0)
        out.append(pltpu.make_async_copy(
            done.at[part], imag_ref if c else real_ref.at[pl.ds(2 * e, 2)], done_sem.at[part]))
        out[-1].start()

    pltpu.make_async_copy(last_ref, last_ref, recv2.at[3]).wait()
    for copy in out:
        copy.wait()
    for e in range(2):
        others = recv.at[e, pl.ds(0, TM - 1)]
        pltpu.make_async_copy(others, others, send1.at[e]).wait()
    own = jnp.logical_or(owner_block(x, core, y, zl, 0) == j, owner_block(x, core, y, zl, 1) == j)

    @pl.when(own)
    def _():
        most = vis.at[:, pl.ds(0, BLOCK * FREQ - 1)]
        pltpu.make_async_copy(most, most, send2).wait()

    @pl.when(jnp.logical_not(own))
    def _():
        pltpu.make_async_copy(vis, vis, send2).wait()


def exchange(classes, vis, power, square, count, mask, bank):
    high, low, twist = dft_tables()
    vmem, hbm = pl.BlockSpec(memory_space=pltpu.VMEM), pl.BlockSpec(memory_space=pl.ANY)
    dma = pltpu.SemaphoreType.DMA
    width = FREQ * CHAN
    return pl.pallas_call(
        exchange_kernel,
        name="exchange",
        out_shape=(
            jax.ShapeDtypeStruct((2, LEN, width), BF),
            jax.ShapeDtypeStruct((BLOCK, width, LEN), BF),
            jax.ShapeDtypeStruct((2, width, LEN), BF),
        ),
        in_specs=[pl.BlockSpec(memory_space=pltpu.SMEM), hbm] + [vmem] * 8 + [hbm],
        out_specs=(hbm, hbm, hbm),
        scratch_shapes=[
            pltpu.VMEM((2, BLOCK * FREQ, CHAN, LEN), BF),
            pltpu.VMEM((CHAN, LEN), F32),
            pltpu.VMEM((2, CHAN, 128), F32),
            pltpu.VMEM((CHAN, LEN), F32),
            pltpu.VMEM((2, TM, 2, CHAN, LEN), BF),
            pltpu.VMEM((TM, CHAN, 2 * LEN), BF),
            pltpu.VMEM((TM, CHAN, 2 * LEN), BF),
            pltpu.VMEM((2, 2, TM, LEN, CHAN), BF),
            pltpu.VMEM((3, 2, LEN, width), BF),
            pltpu.VMEM((4, width, width), BF),
            pltpu.VMEM((LEN, width), BF),
            pltpu.VMEM((3, 2, width, LEN), BF),
            dma((2,)), dma((2,)), dma((2,)), dma((2,)), dma((2,)), dma, dma((4,)), dma((3,)),
        ],
        compiler_params=pltpu.CompilerParams(
            collective_id=0, has_side_effects=True, vmem_limit_bytes=56 << 20),
    )(classes, vis, power, square, count, mask, jnp.asarray(high), jnp.asarray(low), jnp.asarray(twist),
      jnp.asarray(order_table()), bank)


def finish_kernel(class_ref, last_ref, order_ref, bank_hbm, real_hbm, imag_hbm, out_ref, bank, held, done, kept,
                  bank_sem, kept_sem, copy_sem, done_sem):
    loads = []
    for z in range(2):
        for h in range(2):
            rows = pl.ds(512 * h, 512)
            loads.append(pltpu.make_async_copy(
                bank_hbm.at[class_ref[2 + z], rows], bank.at[z, rows], bank_sem.at[z, h]))
            loads[-1].start()
    early = []
    for n in range(BLOCK + 2):
        source = real_hbm.at[n] if n < BLOCK else imag_hbm.at[n - BLOCK]
        early.append(pltpu.make_async_copy(source, kept.at[n], kept_sem.at[n]))
        early[-1].start()
    copies = []
    for z in range(2):
        held[z] = jnp.dot(order_ref[...], last_ref[z], preferred_element_type=F32).astype(BF)
    for n in range(BLOCK + 2):
        early[n].wait()
        copies.append(pltpu.make_async_copy(kept.at[n], out_ref.at[n // BLOCK, n % BLOCK], copy_sem.at[n]))
        copies[-1].start()
    for z in range(2):
        for h in range(2):
            loads[2 * z + h].wait()
            rows = pl.ds(512 * h, 512)
            done[z, rows, :] = lax.dot_general(
                bank[z, rows, :], held[z], (((1,), (1,)), ((), ())), preferred_element_type=F32).astype(BF)
            copies.append(pltpu.make_async_copy(done.at[z, rows], out_ref.at[1, 2 + z, rows], done_sem.at[z, h]))
            copies[-1].start()
    for copy in copies:
        copy.wait()


def finish(classes, last, bank, real, imag):
    width = FREQ * CHAN
    vmem, hbm = pl.BlockSpec(memory_space=pltpu.VMEM), pl.BlockSpec(memory_space=pl.ANY)
    dma = pltpu.SemaphoreType.DMA
    return pl.pallas_call(
        finish_kernel,
        name="finish",
        out_shape=jax.ShapeDtypeStruct((2, BLOCK, width, LEN), BF),
        in_specs=[pl.BlockSpec(memory_space=pltpu.SMEM), vmem, vmem, hbm, hbm, hbm],
        out_specs=hbm,
        scratch_shapes=[
            pltpu.VMEM((2, width, width), BF),
            pltpu.VMEM((2, LEN, width), BF),
            pltpu.VMEM((2, width, LEN), BF),
            pltpu.VMEM((BLOCK + 2, width, LEN), BF),
            dma((2, 2)), dma((BLOCK + 2,)), dma((BLOCK + 2,)), dma((2, 2)),
        ],
        compiler_params=pltpu.CompilerParams(vmem_limit_bytes=60 << 20),
    )(classes, last, jnp.asarray(order_table()), bank, real, imag)


def shards(visibility, power, square, count, mask, classes, bank):
    classes = classes[:, 0]
    last, real, imag = exchange(classes, visibility, power, square, count, mask, bank)
    return finish(classes, last, bank, real, imag)


def solution(mesh):
    in_specs = (
        P(None, None, "freq", "tm"),
        P("freq", "tm"),
        P("freq", "tm"),
        P("freq", "tm"),
        P("freq", "tm"),
        P("freq", None),
        P(),
    )
    out_specs = P(None, "freq", None, "tm")
    return jax.shard_map(shards, mesh=mesh, in_specs=in_specs, out_specs=out_specs, check_vma=False)
```

time: 140 us -> 121 us (0.86)
  Pallas kernels: 134 us -> 121 us
  local copies, waits for them, and re-layouts: 5.57 us -> 0 us
    pallas_call x2, Pallas kernels: 134 us -> 121 us  [the longest x1 112 us: exchange(): pl.pallas_call(exchange_kernel, name='exchange', out_shape=(jax.ShapeDtyp...]
    unnamed x8 -> x0, local copies, waits for them, and re-layouts: 5.57 us -> none
where the time goes in v2:
time: 121 us
  Pallas kernels  121 us (100%)
    pallas_call x1, Pallas kernels, exchange(): pl.pallas_call(exchange_kernel, name='exchange', out_shape=(jax.ShapeDtyp...  112 us
    pallas_call x1, Pallas kernels, finish(): pl.pallas_call(finish_kernel, name='finish', out_shape=jax.ShapeDtypeStru...  8.84 us

profile of v2, /device:TPU:1, one launch (start us, length us, event | category | flops | bytes accessed | tf_op | source)
XLA Modules:
  0.0 121.2 jit_solution(17816188185444124283)
XLA Ops:
  0.0 112.4 %exchange.1 = (bf16[2,256,1024]{2,1,0:T(8,128)(2,1)}, bf16[4,1024,256]{2,1,0:T(8,128)(2,1)}, bf16[2,1024,256]{2,1,0:T(8,128)(2,1)}) custom-call(s32[4]{0:T(128)} %bitcast.1, bf16[2,32,128,256]{3,2,1,0:T(8,128)(2,1)} %vis_hbm.1, f32[128,256]{1,0:T(8,128)} %power_ref.1, f32[128,256]{1,0:T(8,128)} %square_ref.1, s32[128,256]{1,0:T(8,128)} %count_ref.1, ...), custom_call_target="tpu_custom_call" | custom-call | tf_op jit(solution)/shard_map/exchange/pallas_call | solution.py:321
  112.4 8.8 %finish.1 = bf16[2,4,1024,256]{3,2,1,0:T(8,128)(2,1)} custom-call(s32[4]{0:T(128)} %bitcast.2, bf16[2,256,1024]{2,1,0:T(8,128)(2,1)} %get-tuple-element.8.last_ref, bf16[256,256]{1,0:T(8,128)(2,1)} %constant.11.clone.order_ref, bf16[4,1024,1024]{2,1,0:T(8,128)(2,1)} %bank_hbm.3, bf16[4,1024,256]{2,1,0:T(8,128)(2,1)} %get-tuple-element.9.real_hbm, ...), custom_call_target="tpu_custom_call" | custom-call | tf_op jit(solution)/shard_map/finish/pallas_call | solution.py:389

commit v3 on v2

--- a/solution.py
+++ b/solution.py
@@ -17,7 +17,7 @@
 SAMPLES = TM * LEN
 BLOCK = 4
 BF, F32 = jnp.bfloat16, jnp.float32
-PIECES_1, PIECES_2 = 4, 4
+PIECES_1, PIECES_2 = 4, 8
 ORDER_1, ORDER_2 = 11, 21
 OFFSETS = [(a, b, c) for a in range(4) for b in range(2) for c in range(2)]
 
@@ -40,11 +40,10 @@
     return high, low, twist.astype(np.float32)
 
 
-def order_table():
-    m = np.arange(LEN)
-    table = np.zeros((LEN, LEN), np.float32)
-    table[m, (m % TM) * TM + m // TM] = 1.0
-    return table.astype(jnp.bfloat16)
+def row_order():
+    m = lax.broadcasted_iota(jnp.int32, (LEN, LEN), 0)
+    r = lax.broadcasted_iota(jnp.int32, (LEN, LEN), 1)
+    return jnp.where(lax.rem(m, TM) * TM + m // TM == r, 1.0, 0.0).astype(BF)
 
 
 def place(i, j):
@@ -105,10 +104,11 @@
 
 
 def exchange_kernel(
-    class_ref, vis_hbm, power_ref, square_ref, count_ref, mask_ref, high_ref, low_ref, twist_ref, order_ref, bank_hbm,
+    class_ref, vis_hbm, power_hbm, square_hbm, count_hbm, mask_hbm, high_hbm, low_hbm, twist_hbm, bank_hbm,
     last_ref, real_ref, imag_ref,
-    vis, flags, edge, smooth, recv, yhigh, ylow, send, spec, bank, held, done,
-    load_sem, halo_send, halo_recv, send1, recv1, send2, recv2, done_sem,
+    vis, power_ref, square_ref, count_ref, mask_ref, high_ref, low_ref, twist_ref,
+    flags, edge, smooth, recv, yhigh, ylow, send, spec, bank, held, done,
+    load_sem, field_sem, table_sem, halo_send, halo_recv, send1, recv1, send2, recv2, done_sem,
 ):
     i, j = lax.axis_index("tm"), lax.axis_index("freq")
     x, zh, core, y, zl = place(i, j)
@@ -118,9 +118,24 @@
         pl.semaphore_signal(barrier, inc=1, device_id=(lax.rem(i + k, TM), j), device_id_type=MESH)
     for k in range(1, FREQ):
         pl.semaphore_signal(barrier, inc=1, device_id=(i, lax.rem(j + k, FREQ)), device_id_type=MESH)
+    fields = [
+        pltpu.make_async_copy(source, target, field_sem.at[n])
+        for n, (source, target) in enumerate((
+            (count_hbm, count_ref), (power_hbm, power_ref), (square_hbm, square_ref), (mask_hbm, mask_ref)))
+    ]
+    for copy in fields:
+        copy.start()
     load = pltpu.make_async_copy(vis_hbm, vis, load_sem.at[0])
     load.start()
 
+    tables = [
+        pltpu.make_async_copy(source, target, table_sem.at[n])
+        for n, (source, target) in enumerate(((high_hbm, high_ref), (low_hbm, low_ref), (twist_hbm, twist_ref)))
+    ]
+    for copy in tables:
+        copy.start()
+    for copy in fields:
+        copy.wait()
     counts = count_ref[...].astype(F32)
     power = power_ref[...]
     kurtosis = (counts + 1.0) / (counts - 1.0) * (counts * square_ref[...] / (power * power) - 1.0)
@@ -193,6 +208,9 @@
                 hand(e, o, 1, rows)
             return 0
         lax.fori_loop(0, PIECES_1, rest, 0)
+
+    for copy in tables:
+        copy.wait()
 
     for e in range(2):
         others = recv.at[e, pl.ds(0, TM - 1)]
@@ -276,12 +294,13 @@
             lax.fori_loop(0, PIECES_2, share, 0)
 
     bank_load.wait()
+    row_table = row_order()
     out = []
     for part in range(3):
         e, c = part // 2, part % 2
         pltpu.make_async_copy(spec.at[part], spec.at[part], recv2.at[part]).wait()
         for z in range(2):
-            held[...] = jnp.dot(order_ref[...], spec[part, z], preferred_element_type=F32).astype(BF)
+            held[...] = jnp.dot(row_table, spec[part, z], preferred_element_type=F32).astype(BF)
 
             def rows_of(g, _):
                 at = pl.ds(pl.multiple_of(g * 512, 512), 512)
@@ -315,7 +334,7 @@
 
 def exchange(classes, vis, power, square, count, mask, bank):
     high, low, twist = dft_tables()
-    vmem, hbm = pl.BlockSpec(memory_space=pltpu.VMEM), pl.BlockSpec(memory_space=pl.ANY)
+    hbm, anywhere = pl.BlockSpec(memory_space=pltpu.HBM), pl.BlockSpec(memory_space=pl.ANY)
     dma = pltpu.SemaphoreType.DMA
     width = FREQ * CHAN
     return pl.pallas_call(
@@ -326,10 +345,17 @@
             jax.ShapeDtypeStruct((BLOCK, width, LEN), BF),
             jax.ShapeDtypeStruct((2, width, LEN), BF),
         ),
-        in_specs=[pl.BlockSpec(memory_space=pltpu.SMEM), hbm] + [vmem] * 8 + [hbm],
-        out_specs=(hbm, hbm, hbm),
+        in_specs=[pl.BlockSpec(memory_space=pltpu.SMEM)] + [hbm] * 9,
+        out_specs=(anywhere, anywhere, anywhere),
         scratch_shapes=[
             pltpu.VMEM((2, BLOCK * FREQ, CHAN, LEN), BF),
+            pltpu.VMEM((CHAN, LEN), F32),
+            pltpu.VMEM((CHAN, LEN), F32),
+            pltpu.VMEM((CHAN, LEN), jnp.int32),
+            pltpu.VMEM((CHAN, LEN), jnp.int32),
+            pltpu.VMEM((2 * LEN, 2 * LEN), BF),
+            pltpu.VMEM((2 * LEN, 2 * LEN), BF),
+            pltpu.VMEM((2, TM, LEN), F32),
             pltpu.VMEM((CHAN, LEN), F32),
             pltpu.VMEM((2, CHAN, 128), F32),
             pltpu.VMEM((CHAN, LEN), F32),
@@ -341,41 +367,29 @@
             pltpu.VMEM((4, width, width), BF),
             pltpu.VMEM((LEN, width), BF),
             pltpu.VMEM((3, 2, width, LEN), BF),
-            dma((2,)), dma((2,)), dma((2,)), dma((2,)), dma((2,)), dma, dma((4,)), dma((3,)),
+            dma((2,)), dma((4,)), dma((3,)), dma((2,)), dma((2,)), dma((2,)), dma((2,)), dma, dma((4,)), dma((3,)),
         ],
         compiler_params=pltpu.CompilerParams(
-            collective_id=0, has_side_effects=True, vmem_limit_bytes=56 << 20),
-    )(classes, vis, power, square, count, mask, jnp.asarray(high), jnp.asarray(low), jnp.asarray(twist),
-      jnp.asarray(order_table()), bank)
-
-
-def finish_kernel(class_ref, last_ref, order_ref, bank_hbm, real_hbm, imag_hbm, out_ref, bank, held, done, kept,
-                  bank_sem, kept_sem, copy_sem, done_sem):
-    loads = []
+            collective_id=0, has_side_effects=True, vmem_limit_bytes=47 << 20),
+    )(classes, *(pltpu.with_memory_space_constraint(value, pltpu.HBM) for value in (
+        vis, power, square, count, mask, jnp.asarray(high), jnp.asarray(low), jnp.asarray(twist), bank)))
+
+
+def finish_kernel(class_ref, last_ref, bank_ref, real_ref, imag_ref, out_ref, held, done, copy_sem, done_sem):
+    copies = []
+    for n in range(BLOCK + 2):
+        source = real_ref.at[n] if n < BLOCK else imag_ref.at[n - BLOCK]
+        copies.append(pltpu.make_async_copy(source, out_ref.at[n // BLOCK, n % BLOCK], copy_sem.at[n]))
+        copies[-1].start()
+    row_table = row_order()
+    for z in range(2):
+        held[z] = jnp.dot(row_table, last_ref[z], preferred_element_type=F32).astype(BF)
     for z in range(2):
         for h in range(2):
             rows = pl.ds(512 * h, 512)
-            loads.append(pltpu.make_async_copy(
-                bank_hbm.at[class_ref[2 + z], rows], bank.at[z, rows], bank_sem.at[z, h]))
-            loads[-1].start()
-    early = []
-    for n in range(BLOCK + 2):
-        source = real_hbm.at[n] if n < BLOCK else imag_hbm.at[n - BLOCK]
-        early.append(pltpu.make_async_copy(source, kept.at[n], kept_sem.at[n]))
-        early[-1].start()
-    copies = []
-    for z in range(2):
-        held[z] = jnp.dot(order_ref[...], last_ref[z], preferred_element_type=F32).astype(BF)
-    for n in range(BLOCK + 2):
-        early[n].wait()
-        copies.append(pltpu.make_async_copy(kept.at[n], out_ref.at[n // BLOCK, n % BLOCK], copy_sem.at[n]))
-        copies[-1].start()
-    for z in range(2):
-        for h in range(2):
-            loads[2 * z + h].wait()
-            rows = pl.ds(512 * h, 512)
             done[z, rows, :] = lax.dot_general(
-                bank[z, rows, :], held[z], (((1,), (1,)), ((), ())), preferred_element_type=F32).astype(BF)
+                bank_ref[class_ref[2 + z], rows, :], held[z], (((1,), (1,)), ((), ())),
+                preferred_element_type=F32).astype(BF)
             copies.append(pltpu.make_async_copy(done.at[z, rows], out_ref.at[1, 2 + z, rows], done_sem.at[z, h]))
             copies[-1].start()
     for copy in copies:
@@ -390,17 +404,15 @@
         finish_kernel,
         name="finish",
         out_shape=jax.ShapeDtypeStruct((2, BLOCK, width, LEN), BF),
-        in_specs=[pl.BlockSpec(memory_space=pltpu.SMEM), vmem, vmem, hbm, hbm, hbm],
+        in_specs=[pl.BlockSpec(memory_space=pltpu.SMEM)] + [vmem] * 4,
         out_specs=hbm,
         scratch_shapes=[
-            pltpu.VMEM((2, width, width), BF),
             pltpu.VMEM((2, LEN, width), BF),
             pltpu.VMEM((2, width, LEN), BF),
-            pltpu.VMEM((BLOCK + 2, width, LEN), BF),
-            dma((2, 2)), dma((BLOCK + 2,)), dma((BLOCK + 2,)), dma((2, 2)),
+            dma((BLOCK + 2,)), dma((2, 2)),
         ],
-        compiler_params=pltpu.CompilerParams(vmem_limit_bytes=60 << 20),
-    )(classes, last, jnp.asarray(order_table()), bank, real, imag)
+        compiler_params=pltpu.CompilerParams(vmem_limit_bytes=20 << 20),
+    )(classes, last, bank, real, imag)
 
 
 def shards(visibility, power, square, count, mask, classes, bank):

time: 121 us -> 115 us (0.950)
  Pallas kernels: 121 us -> 113 us
    pallas_call x1, Pallas kernels: 8.84 us -> 2.97 us  [finish(): pl.pallas_call(finish_kernel, name='finish', out_shape=jax.ShapeDtypeStru...]
    pallas_call x1, Pallas kernels: 112 us -> 111 us  [exchange(): pl.pallas_call(exchange_kernel, name='exchange', out_shape=(jax.ShapeDtyp...]
where the time goes in v3:
time: 115 us; the launch traced here: 114 us
  Pallas kernels  113 us (98%)
    pallas_call x1, Pallas kernels, exchange(): pl.pallas_call(exchange_kernel, name='exchange', out_shape=(jax.ShapeDtyp...  111 us
    pallas_call x1, Pallas kernels, finish(): pl.pallas_call(finish_kernel, name='finish', out_shape=jax.ShapeDtypeStru...  2.97 us

profile of v3, /device:TPU:1, one launch (start us, length us, event | category | flops | bytes accessed | tf_op | source)
XLA Modules:
  0.0 114.1 jit_solution(8951963961314210621)
XLA Ops:
  0.0 0.0 copy-start.1
  0.0 0.7 copy-done.1
  0.7 0.0 copy-start
  0.7 110.5 %exchange.1 = (bf16[2,256,1024]{2,1,0:T(8,128)(2,1)S(1)}, bf16[4,1024,256]{2,1,0:T(8,128)(2,1)S(1)}, bf16[2,1024,256]{2,1,0:T(8,128)(2,1)S(1)}) custom-call(s32[4]{0:T(128)S(1)} %bitcast.1, bf16[2,32,128,256]{3,2,1,0:T(8,128)(2,1)} %vis_hbm.1, f32[128,256]{1,0:T(8,128)} %power_hbm.1, f32[128,256]{1,0:T(8,128)} %square_hbm.1, s32[128,256]{1,0:T(8,128)} %count_hbm.1, ...), custom_call_target="tpu_custom_call" | custom-call | tf_op jit(solution)/shard_map/exchange/pallas_call | solution.py:340
  111.2 0.0 copy-done
  111.2 3.0 %finish.1 = bf16[2,4,1024,256]{3,2,1,0:T(8,128)(2,1)} custom-call(s32[4]{0:T(128)S(1)} %bitcast.2, bf16[2,256,1024]{2,1,0:T(8,128)(2,1)S(1)} %get-tuple-element.8.last_ref, bf16[4,1024,1024]{2,1,0:T(8,128)(2,1)S(1)} %copy-done, bf16[4,1024,256]{2,1,0:T(8,128)(2,1)S(1)} %get-tuple-element.9.real_ref, bf16[2,1024,256]{2,1,0:T(8,128)(2,1)S(1)} %get-tuple-element.10.imag_ref), custom_call_target="tpu_custom_call" | custom-call | tf_op jit(solution)/shard_map/finish/pallas_call | solution.py:403
Async XLA Ops:
  0.0 0.7 copy-start.1
  0.7 110.5 %copy-start = (bf16[4,1024,1024]{2,1,0:T(8,128)(2,1)S(1)}, bf16[4,1024,1024]{2,1,0:T(8,128)(2,1)}, u32[]{:S(2)}) copy-start(bf16[4,1024,1024]{2,1,0:T(8,128)(2,1)} %bank_ref.1) | copy-start | bytes 25165828

commit v4 on v3

--- a/solution.py
+++ b/solution.py
@@ -18,7 +18,7 @@
 BLOCK = 4
 BF, F32 = jnp.bfloat16, jnp.float32
 PIECES_1, PIECES_2 = 4, 8
-ORDER_1, ORDER_2 = 11, 21
+ORDER_1, ORDER_2 = 30, 21
 OFFSETS = [(a, b, c) for a in range(4) for b in range(2) for c in range(2)]
 
 

time: 115 us -> 115 us (level)
  no operation moved by 1% of the time
where the time goes in v4:
time: 115 us
  Pallas kernels  114 us (99%)
    pallas_call x1, Pallas kernels, exchange(): pl.pallas_call(exchange_kernel, name='exchange', out_shape=(jax.ShapeDtyp...  111 us
    pallas_call x1, Pallas kernels, finish(): pl.pallas_call(finish_kernel, name='finish', out_shape=jax.ShapeDtypeStru...  2.97 us

profile of v4, /device:TPU:1, one launch (start us, length us, event | category | flops | bytes accessed | tf_op | source)
XLA Modules:
  0.0 114.6 jit_solution(2584074025727618592)
XLA Ops:
  0.0 0.0 copy-start.1
  0.0 0.7 copy-done.1
  0.7 0.0 copy-start
  0.7 111.0 %exchange.1 = (bf16[2,256,1024]{2,1,0:T(8,128)(2,1)S(1)}, bf16[4,1024,256]{2,1,0:T(8,128)(2,1)S(1)}, bf16[2,1024,256]{2,1,0:T(8,128)(2,1)S(1)}) custom-call(s32[4]{0:T(128)S(1)} %bitcast.1, bf16[2,32,128,256]{3,2,1,0:T(8,128)(2,1)} %vis_hbm.1, f32[128,256]{1,0:T(8,128)} %power_hbm.1, f32[128,256]{1,0:T(8,128)} %square_hbm.1, s32[128,256]{1,0:T(8,128)} %count_hbm.1, ...), custom_call_target="tpu_custom_call" | custom-call | tf_op jit(solution)/shard_map/exchange/pallas_call | solution.py:340
  111.7 0.0 copy-done
  111.7 3.0 %finish.1 = bf16[2,4,1024,256]{3,2,1,0:T(8,128)(2,1)} custom-call(s32[4]{0:T(128)S(1)} %bitcast.2, bf16[2,256,1024]{2,1,0:T(8,128)(2,1)S(1)} %get-tuple-element.8.last_ref, bf16[4,1024,1024]{2,1,0:T(8,128)(2,1)S(1)} %copy-done, bf16[4,1024,256]{2,1,0:T(8,128)(2,1)S(1)} %get-tuple-element.9.real_ref, bf16[2,1024,256]{2,1,0:T(8,128)(2,1)S(1)} %get-tuple-element.10.imag_ref), custom_call_target="tpu_custom_call" | custom-call | tf_op jit(solution)/shard_map/finish/pallas_call | solution.py:403
Async XLA Ops:
  0.0 0.7 copy-start.1
  0.7 111.0 %copy-start = (bf16[4,1024,1024]{2,1,0:T(8,128)(2,1)S(1)}, bf16[4,1024,1024]{2,1,0:T(8,128)(2,1)}, u32[]{:S(2)}) copy-start(bf16[4,1024,1024]{2,1,0:T(8,128)(2,1)} %bank_ref.1) | copy-start | bytes 25165828
